TPU v7x, 128 devices: a whole 4x4x4 slice. The times are simulated.
128 devices in a mesh: batch: 4 (over y_lo, core), tensor: 8 (over x, y_hi), latent: 4 (over z).
Axes of the slice: x: 4, y: 4 (y_hi: 2, y_lo: 2; y = y_hi * 2 + y_lo), z: 4, core: 2. Of those that a mesh axis runs over, the one named last changes fastest.
Arguments:
- residual: bfloat16 [1024, 3584], P('batch', ('tensor', 'latent')), may hold values from -6 to 6
- target: bfloat16 [1024, 3584], P('batch', ('tensor', 'latent')), may hold values from -6 to 6
- encoder_weight: bfloat16 [3584, 32768], P(None, ('tensor', 'latent')), may hold values from -0.09375 to 0.09375
- encoder_bias: bfloat16 [32768], P(('tensor', 'latent')), may hold values from -0.59765625 to 0.29882812
- decoder_weight: bfloat16 [32768, 3584], P(('tensor', 'latent')), may hold values from -0.09375 to 0.09375
- decoder_bias: bfloat16 [3584], replicated, may hold values from -3 to 3
- first_gain: bfloat16 [3584], replicated, may hold values from 0.5 to 1.5
- second_gain: bfloat16 [3584], replicated, may hold values from 0.5 to 1.5
- gate_weight: bfloat16 [3584, 7168], P(None, ('tensor', 'latent')), may hold values from -0.09375 to 0.09375
- up_weight: bfloat16 [3584, 7168], P(None, ('tensor', 'latent')), may hold values from -0.09375 to 0.09375
- down_weight: bfloat16 [7168, 3584], P(('tensor', 'latent')), may hold values from -0.125 to 0.125
Outputs:
- encoder_grad: bfloat16 [3584, 32768], P('batch', ('tensor', 'latent'))
- decoder_grad: bfloat16 [32768, 3584], P(('tensor', 'latent'), 'batch')
All inputs are finite; a program needn't handle non-finite values.
Results may differ from a plain program's by a relative error of at most 0.012.
The roundings to bfloat16 on the way count: a program that leaves them out, or rounds other values in their place, can miss the bound.
Values may be sent and summed in bfloat16 or wider, within the bound.
No kernel may reach another device: no remote copies, remote signals or barrier semaphores. Data moves between devices by JAX's collectives and lax.ppermute only.
A program may use at most 128 MiB of HBM per device.

v0:
```python
import jax
import jax.numpy as jnp
from jax import lax
from jax.sharding import Mesh
from jax.sharding import PartitionSpec as P

TENSOR_LATENT = ("tensor_0", "tensor_1", "latent")
epsilon = 1e-06


def rows_for(lines, count):
    spare = -len(lines) % count
    return jnp.pad(lines, [(0, spare)] + [(0, 0)] * (lines.ndim - 1))


def copy_for_each(shard, axis):
    copies = jnp.broadcast_to(shard, (lax.axis_size(axis), *shard.shape))
    return lax.all_to_all(copies, axis, split_axis=0, concat_axis=0, tiled=True)


def laid_out(pieces, dim):
    pieces = jnp.moveaxis(pieces, 0, dim)
    lengths = pieces.shape
    return pieces.reshape(*lengths[:dim], lengths[dim] * lengths[dim + 1], *lengths[dim + 2 :])


def whole_of(shard, axes, dim):
    far, near = axes
    initial = copy_for_each(shard, far)
    pieces = jnp.swapaxes(copy_for_each(initial, near), 0, 1)
    return laid_out(pieces.reshape(-1, *shard.shape), dim)


def split_up(shard, dim, count):
    lengths = shard.shape
    pieces = shard.reshape(*lengths[:dim], count, lengths[dim] // count, *lengths[dim + 1 :])
    return jnp.moveaxis(pieces, dim, 0)


def sum_at_owner(shard, axis, dim):
    pieces = split_up(shard, dim, lax.axis_size(axis))
    arrived = lax.all_to_all(pieces, axis, split_axis=0, concat_axis=0, tiled=True)
    return arrived.astype(jnp.float32).sum(axis=0)


def summed_rows(shard, axes, dim):
    far, near = axes
    own = sum_at_owner(split_up(shard, dim, lax.axis_size(far)), near, dim + 1)
    return jnp.sum(
        lax.all_to_all(own.astype(jnp.bfloat16), far, 0, 0, tiled=True).astype(jnp.float32), axis=0
    )


def total_of(shard, axes):
    lines = shard.reshape(-1, shard.shape[-1])
    padded = rows_for(lines, lax.axis_size(axes[0]) * lax.axis_size(axes[1]))
    whole = whole_of(summed_rows(padded, axes, 0).astype(jnp.bfloat16), axes, 0)
    return lax.slice_in_dim(whole, 0, len(lines)).reshape(shard.shape).astype(jnp.float32)


def sum_in_order(pieces, axes, order):
    inside = pieces.shape[1:]
    pieces = pieces.reshape(*(lax.axis_size(a) for a in axes), *inside)
    pieces = jnp.moveaxis(pieces, order, range(len(axes))).reshape(-1, *inside)
    for k in order:
        pieces = lax.psum_scatter(pieces, axes[k], scatter_dimension=0, tiled=True)
    return pieces[0]


def summed_rows_2(shard, axes, order, dim):
    count = lax.axis_size(axes)
    return sum_in_order(split_up(shard, dim, count), axes, order)


def over_copies(shard, axis):
    return copy_for_each(shard, axis).sum(axis=0)


def in_one_piece(arrays, axis, dim, along):
    both = jnp.concatenate(arrays, axis=along)
    out, at, gathered = (lax.all_gather(both, axis, axis=dim, tiled=True), 0, [])
    for a in arrays:
        gathered.append(lax.slice_in_dim(out, at, at + a.shape[along], axis=along))
        at += a.shape[along]
    return tuple(gathered)


def per_device(
    residual,
    target,
    encoder_weight,
    encoder_bias,
    decoder_weight,
    decoder_bias,
    first_gain,
    second_gain,
    gate_weight,
    up_weight,
    down_weight,
):
    f32 = jnp.float32
    bf16 = jnp.bfloat16
    contract_last = (((1,), (1,)), ((), ()))
    contract_first = (((0,), (0,)), ((), ()))
    share_width = residual.shape[1]
    model_width = share_width * lax.axis_size(TENSOR_LATENT)
    offset = lax.axis_index(TENSOR_LATENT) * share_width
    token_count = residual.shape[0] * lax.axis_size("batch")
    bias_share = lax.dynamic_slice_in_dim(decoder_bias.astype(f32), offset, share_width)
    first_share = lax.dynamic_slice_in_dim(first_gain.astype(f32), offset, share_width)
    second_share = lax.dynamic_slice_in_dim(second_gain.astype(f32), offset, share_width)
    centered_share = (residual.astype(f32) - bias_share).astype(bf16)
    centered = lax.all_gather(centered_share, TENSOR_LATENT, axis=1, tiled=True)
    preact = jnp.dot(centered, encoder_weight, preferred_element_type=f32) + encoder_bias.astype(
        f32
    )
    latents = jnp.maximum(preact, 0.0).astype(bf16)
    partial_recon = jnp.dot(latents, decoder_weight, preferred_element_type=f32)
    recon_full = total_of(
        partial_recon.astype(jnp.bfloat16), (("tensor_0", "tensor_1"), "latent")
    ) + decoder_bias.astype(f32)
    scale_in = lax.rsqrt(
        jnp.sum(recon_full * recon_full, axis=1, keepdims=True) / model_width + epsilon
    )
    normed_input = (recon_full * scale_in * first_gain.astype(f32)).astype(bf16)
    recon = lax.dynamic_slice_in_dim(recon_full, offset, share_width, 1)
    gate_value = jnp.dot(normed_input, gate_weight, preferred_element_type=f32)
    up_value = jnp.dot(normed_input, up_weight, preferred_element_type=f32)
    gelu_value, gelu_back = jax.vjp(lambda v: jax.nn.gelu(v, approximate=True), gate_value)
    hidden = (gelu_value * up_value).astype(bf16)
    partial_out = jnp.dot(hidden, down_weight, preferred_element_type=f32)
    output = summed_rows_2(partial_out.astype(jnp.bfloat16), TENSOR_LATENT, (0, 2, 1), 1).astype(
        jnp.float32
    )
    out_squares = over_copies(jnp.sum(output * output, axis=1), TENSOR_LATENT)
    scale_out = lax.rsqrt(out_squares[:, None] / model_width + epsilon)
    normed_out = output * scale_out
    result = recon + normed_out * second_share
    grad_result = 2.0 * (result - target.astype(f32)) / token_count
    grad_normed = grad_result * second_share
    inner_out = over_copies(jnp.sum(grad_normed * normed_out, axis=1), TENSOR_LATENT) / model_width
    grad_share = (scale_out * (grad_normed - normed_out * inner_out[:, None])).astype(bf16)
    grad_output = lax.all_gather(grad_share, TENSOR_LATENT, axis=1, tiled=True)
    grad_hidden = lax.dot_general(
        grad_output, down_weight, contract_last, preferred_element_type=f32
    )
    grad_gate = gelu_back(grad_hidden * up_value)[0].astype(bf16)
    grad_up = (grad_hidden * gelu_value).astype(bf16)
    partial_input = lax.dot_general(
        grad_gate, gate_weight, contract_last, preferred_element_type=f32
    )
    partial_input = partial_input + lax.dot_general(
        grad_up, up_weight, contract_last, preferred_element_type=f32
    )
    grad_normed_in = sum_at_owner(partial_input.astype(jnp.bfloat16), TENSOR_LATENT, 1)
    unit = recon * scale_in
    grad_unit = grad_normed_in * first_share
    inner_in = over_copies(jnp.sum(grad_unit * unit, axis=1), TENSOR_LATENT) / model_width
    recon_share = (grad_result + scale_in * (grad_unit - unit * inner_in[:, None])).astype(bf16)
    grad_recon = lax.all_gather(recon_share, TENSOR_LATENT, axis=1, tiled=True)
    grad_latent = lax.dot_general(
        grad_recon, decoder_weight, contract_last, preferred_element_type=f32
    )
    grad_preact = jnp.where(preact > 0, grad_latent, 0.0).astype(bf16)
    centered_block, recon_block = (
        lax.all_to_all(centered, "batch", split_axis=1, concat_axis=0, tiled=True),
        lax.all_to_all(grad_recon, "batch", split_axis=1, concat_axis=0, tiled=True),
    )
    latents_all, preact_all = in_one_piece((latents, grad_preact), "batch", 0, 1)
    encoder_grad = lax.dot_general(
        centered_block, preact_all, contract_first, preferred_element_type=f32
    )
    decoder_grad = lax.dot_general(
        latents_all, recon_block, contract_first, preferred_element_type=f32
    )
    return (encoder_grad.astype(bf16), decoder_grad.astype(bf16))


def solution(mesh):
    split = Mesh(
        mesh.devices.reshape(mesh.shape["batch"], 4, 2, mesh.shape["latent"]),
        ("batch", "tensor_0", "tensor_1", "latent"),
    )
    in_specs = (
        P("batch", TENSOR_LATENT),
        P("batch", TENSOR_LATENT),
        P(None, TENSOR_LATENT),
        P(TENSOR_LATENT),
        P(TENSOR_LATENT, None),
        P(),
        P(),
        P(),
        P(None, TENSOR_LATENT),
        P(None, TENSOR_LATENT),
        P(TENSOR_LATENT, None),
    )
    out_specs = (P("batch", TENSOR_LATENT), P(TENSOR_LATENT, "batch"))
    return jax.shard_map(
        per_device, mesh=split, in_specs=in_specs, out_specs=out_specs, check_vma=False
    )
```

profile of v0, /device:TPU:1, one launch (start us, length us, event | category | flops | bytes accessed | tf_op | source)
XLA Modules:
  0.0 584.4 jit_solution(9790143516048892075)
XLA Ops:
  7.2 0.9 dynamic_slice.12
  8.1 1.5 subtract_convert_fusion
  9.7 0.7 convert_element_type.91
  10.3 72.6 %all-gather.5.cloned.1.call-done = bf16[256,3584]{0,1:T(8,128)(2,1)} async-done(((bf16[256,112]{0,1:T(8,128)(2,1)}), bf16[256,3584]{0,1:T(8,128)(2,1)}) %all-gather.5.cloned.1.call-update) | async-done | bytes 1835024 | tf_op jit(solution)/shard_map/all_gather | solution.py:113
  82.9 6.7 %maximum_convert_fusion = (bf16[256,1024]{1,0:T(8,128)(2,1)S(1)}, f32[256,1024]{1,0:T(8,128)}) fusion(f32[1024]{0:T(1024)S(1)} %convert_element_type.91, bf16[256,3584]{0,1:T(8,128)(2,1)} %all-gather.5.cloned.1.call-done, bf16[3584,1024]{1,0:T(8,128)(2,1)} %param.13), kind=kOutput, calls=%fused_computation.20 | convolution fusion | flops 1879834624 | bytes 10752000 | tf_op jit(solution)/shard_map/dot_general | solution.py:114
  89.7 5.3 convolution_convert_fusion
  95.0 0.1 copy.66
  95.2 23.6 %all_to_all.81 = bf16[4,8,8,3584]{3,2,1,0:T(8,128)(2,1)S(1)} all-to-all(bf16[4,8,8,3584]{3,2,1,0:T(8,128)(2,1)S(1)} %bitcast.58), channel_id=1, replica_groups=mesh['batch'=4,'tensor_0'=4,'tensor_1'=2,'latent'=4] {'latent'}, dimensions={0} | all-to-all | bytes 3670016 | tf_op jit(solution)/shard_map/all_to_all | solution.py:42
  118.8 1.1 reduce_sum.98
  119.9 11.9 %all_to_all.82 = bf16[8,8,3584]{2,1,0:T(8,128)(2,1)S(1)} all-to-all(bf16[8,8,3584]{2,1,0:T(8,128)(2,1)} %reduce_sum.98), channel_id=1, replica_groups=mesh['batch'=4,'tensor_0'=4,'tensor_1'=2,'latent'=4] {'tensor_0','tensor..., dimensions={0} | all-to-all | bytes 917504 | tf_op jit(solution)/shard_map/all_to_all | solution.py:50
  131.8 0.1 reduce_sum.99
  131.9 11.1 %all_to_all.83 = bf16[8,8,3584]{2,1,0:T(8,128)(2,1)S(1)} all-to-all(bf16[8,8,3584]{2,1,0:T(8,128)(2,1)S(1)} %broadcast_in_dim.11), channel_id=1, replica_groups=mesh['batch'=4,'tensor_0'=4,'tensor_1'=2,'latent'=4] {'tensor_0','tensor..., dimensions={0} | all-to-all | bytes 917504 | tf_op jit(solution)/shard_map/all_to_all | solution.py:18
  143.1 1.4 broadcast_in_dim.12
  144.4 3.7 all-to-all-start.4
  148.2 17.5 %all-to-all-done.4 = bf16[4,8,8,3584]{3,2,1,0:T(8,128)(2,1)S(1)} async-done(((bf16[4,8,8,3584]{3,2,1,0:T(8,128)(2,1)}), bf16[4,8,8,3584]{3,2,1,0:T(8,128)(2,1)S(1)}, u32[]{:S(2)}, u32[]{:S(2)}) %all-to-all-start.4) | async-done | bytes 1835040 | tf_op jit(solution)/shard_map/all_to_all | solution.py:18
  165.8 2.2 copy_convert_fusion
  168.0 5.1 copy.51
  173.2 4.4 broadcast_add_fusion
  177.6 0.6 multiply_reduce_fusion
  178.2 0.1 rsqrt.20
  178.3 3.5 fusion.51
  181.7 0.1 copy-done.2
  181.9 0.5 copy-done.5
  182.4 0.8 fusion.52
  183.2 0.7 copy-done.12
  183.8 1.9 convolution_convert_fusion.1
  185.8 2.9 copy.52
  188.7 1.4 copy.53
  190.2 29.4 %reduce-scatter.4.cloned.1.call-done = bf16[8,256,112]{1,2,0:T(8,128)(2,1)} async-done(((bf16[32,256,112]{1,2,0:T(8,128)(2,1)}), bf16[8,256,112]{1,2,0:T(8,128)(2,1)}) %reduce-scatter.4.cloned.1.call-update) | async-done | bytes 458768 | tf_op jit(solution)/shard_map/reduce_scatter | solution.py:66
  219.7 21.8 %reduce-scatter.6.cloned.1.call-done = bf16[2,256,112]{1,2,0:T(8,128)(2,1)} async-done(((bf16[8,256,112]{1,2,0:T(8,128)(2,1)}), bf16[2,256,112]{1,2,0:T(8,128)(2,1)}) %reduce-scatter.6.cloned.1.call-update) | async-done | bytes 114704 | tf_op jit(solution)/shard_map/reduce_scatter | solution.py:66
  241.5 17.6 %reduce-scatter.8.cloned.1.call-done = bf16[1,256,112]{1,2,0:T(8,128)(2,1)} async-done(((bf16[2,256,112]{1,2,0:T(8,128)(2,1)}), bf16[1,256,112]{1,2,0:T(8,128)(2,1)}) %reduce-scatter.8.cloned.1.call-update) | async-done | bytes 57360 | tf_op jit(solution)/shard_map/reduce_scatter | solution.py:66
  259.0 0.8 fusion.28
  259.9 0.6 broadcast_in_dim.13
  260.5 7.0 %all-to-all-start.5 = ((f32[32,1,256]{2,1,0:T(1,128)}), f32[32,1,256]{2,1,0:T(1,128)S(1)}, u32[]{:S(2)}, u32[]{:S(2)}) async-start(f32[32,1,256]{2,1,0:T(1,128)} %broadcast_in_dim.13), calls=%async_computation.8 | async-start | bytes 65536 | tf_op jit(solution)/shard_map/all_to_all | solution.py:18
  267.6 0.8 broadcast_multiply_fusion.2
  268.3 7.9 %all-to-all-done.5 = f32[32,1,256]{2,1,0:T(1,128)S(1)} async-done(((f32[32,1,256]{2,1,0:T(1,128)}), f32[32,1,256]{2,1,0:T(1,128)S(1)}, u32[]{:S(2)}, u32[]{:S(2)}) %all-to-all-start.5) | async-done | bytes 32800 | tf_op jit(solution)/shard_map/all_to_all | solution.py:18
  276.2 0.1 reduce_sum.103
  276.3 1.1 fusion.24
  277.4 12.1 %all_to_all.84 = f32[32,1,256]{2,1,0:T(1,128)S(1)} all-to-all(f32[32,1,256]{2,1,0:T(1,128)S(1)} %broadcast_in_dim.14), channel_id=1, replica_groups=mesh['batch'=4,'tensor_0'=4,'tensor_1'=2,'latent'=4] {'tensor_0','tensor..., dimensions={0} | all-to-all | bytes 65536 | tf_op jit(solution)/shard_map/all_to_all | solution.py:18
  289.5 1.7 fusion.27
  291.2 66.7 %all-gather.7.cloned.1.call-done = bf16[256,3584]{0,1:T(8,128)(2,1)} async-done(((bf16[256,112]{0,1:T(8,128)(2,1)}), bf16[256,3584]{0,1:T(8,128)(2,1)}) %all-gather.7.cloned.1.call-update) | async-done | bytes 1835024 | tf_op jit(solution)/shard_map/all_gather | solution.py:143
  357.9 2.1 fusion.53
  360.1 0.8 fusion.29
  360.9 0.6 copy-done.6
  361.5 0.7 fusion
  362.2 2.3 copy.56
  364.5 4.1 all-to-all-start.7
  368.7 0.1 dynamic_slice.15
  368.8 22.6 %all-to-all-done.7 = bf16[32,256,112]{1,2,0:T(8,128)(2,1)S(1)} async-done(((bf16[32,256,112]{1,2,0:T(8,128)(2,1)}), bf16[32,256,112]{1,2,0:T(8,128)(2,1)S(1)}, u32[]{:S(2)}, u32[]{:S(2)}) %all-to-all-start.7) | async-done | bytes 1835040 | tf_op jit(solution)/shard_map/all_to_all | solution.py:42
  391.3 0.3 convert_reduce_fusion
  391.6 1.0 multiply_reduce_fusion.1
  392.6 16.3 %all_to_all.85 = f32[32,1,256]{2,1,0:T(1,128)S(1)} all-to-all(f32[32,1,256]{2,1,0:T(1,128)S(1)} %broadcast_in_dim.15), channel_id=1, replica_groups=mesh['batch'=4,'tensor_0'=4,'tensor_1'=2,'latent'=4] {'tensor_0','tensor..., dimensions={0} | all-to-all | bytes 65536 | tf_op jit(solution)/shard_map/all_to_all | solution.py:18
  408.9 1.6 add_convert_fusion
  410.6 66.5 %all-gather.9.cloned.1.call-done = bf16[256,3584]{0,1:T(8,128)(2,1)} async-done(((bf16[256,112]{0,1:T(8,128)(2,1)}), bf16[256,3584]{0,1:T(8,128)(2,1)}) %all-gather.9.cloned.1.call-update) | async-done | bytes 1835024 | tf_op jit(solution)/shard_map/all_gather | solution.py:160
  477.1 5.8 fusion.11
  483.0 1.1 pad_maximum_fusion
  484.0 0.8 copy-done.3
  484.8 44.0 %all_to_all.86 = bf16[256,4,896]{0,2,1:T(8,128)(2,1)} all-to-all(bf16[256,4,896]{0,2,1:T(8,128)(2,1)S(1)} %bitcast.54), channel_id=1, replica_groups=mesh['batch'=4,'tensor_0'=4,'tensor_1'=2,'latent'=4] {'batch'}, dimensions={1} | all-to-all | bytes 3670016 | tf_op jit(solution)/shard_map/all_to_all | solution.py:166
  528.8 5.0 all-to-all-start.9
  533.8 3.5 copy.48
  537.4 28.5 %all-to-all-done.9 = bf16[256,4,896]{0,2,1:T(8,128)(2,1)S(1)} async-done(((bf16[256,4,896]{0,2,1:T(8,128)(2,1)}), bf16[256,4,896]{0,2,1:T(8,128)(2,1)S(1)}, u32[]{:S(2)}, u32[]{:S(2)}) %all-to-all-start.9) | async-done | bytes 1835040 | tf_op jit(solution)/shard_map/all_to_all | solution.py:167
  565.9 2.4 copy.58
  568.3 5.9 %fusion.8 = bf16[1024,896]{1,0:T(8,128)(2,1)} fusion(bf16[1024,896]{1,0:T(8,128)(2,1)} %bitcast.62, bf16[1024,2048]{1,0:T(8,128)(2,1)} %all-gather.11.cloned.1.call-done), kind=kOutput, calls=%fused_computation.15 | convolution fusion | flops 1879965696 | bytes 5767168 | tf_op jit(solution)/shard_map/dot_general | solution.py:173
  574.2 3.4 fusion.5
  (63 shorter events, 0.7 us)
Async XLA Ops:
  7.2 176.7 %copy-start = (bf16[224,3584]{1,0:T(8,128)(2,1)S(1)}, bf16[224,3584]{1,0:T(8,128)(2,1)}, u32[]{:S(2)}) copy-start(bf16[224,3584]{1,0:T(8,128)(2,1)} %param.21) | copy-start | bytes 4816900
  7.2 75.8 %all-gather.5.cloned.1.call-start = ((), (), s32[]{:S(2)}) async-start(), calls=%async_computation.13 | async-start | bytes 1892352 | tf_op jit(solution)/shard_map/all_gather | solution.py:113
  89.7 5.4 copy-start.10
  144.4 3.8 copy-start.18
  144.4 3.8 copy-start.19
  144.4 21.3 %all-to-all-start.4 = ((bf16[4,8,8,3584]{3,2,1,0:T(8,128)(2,1)}), bf16[4,8,8,3584]{3,2,1,0:T(8,128)(2,1)S(1)}, u32[]{:S(2)}, u32[]{:S(2)}) async-start(bf16[4,8,8,3584]{3,2,1,0:T(8,128)(2,1)} %broadcast_in_dim.12), calls=%async_computation.4 | async-start | bytes 3670016 | tf_op jit(solution)/shard_map/all_to_all | solution.py:18
  148.2 71.4 %reduce-scatter.4.cloned.1.call-start = ((), (), s32[]{:S(2)}) async-start(), calls=%async_computation.14 | async-start | bytes 2293760 | tf_op jit(solution)/shard_map/reduce_scatter | solution.py:66
  178.2 3.6 copy-start.2
  178.3 4.1 copy-start.5
  182.3 0.8 copy-start.7
  183.1 0.7 copy-start.12
  190.1 86.2 %copy-start.17 = (bf16[256,112]{0,1:T(8,128)(2,1)S(1)}, bf16[256,112]{0,1:T(8,128)(2,1)}, u32[]{:S(2)}) copy-start(bf16[256,112]{0,1:T(8,128)(2,1)} %param.12) | copy-start | bytes 172036
  190.1 51.3 %reduce-scatter.6.cloned.1.call-start = ((), (), s32[]{:S(2)}) async-start(), calls=%async_computation.15 | async-start | bytes 573440 | tf_op jit(solution)/shard_map/reduce_scatter | solution.py:66
  219.6 39.4 %reduce-scatter.8.cloned.1.call-start = ((), (), s32[]{:S(2)}) async-start(), calls=%async_computation.16 | async-start | bytes 172032 | tf_op jit(solution)/shard_map/reduce_scatter | solution.py:66
  260.5 15.7 %all-to-all-start.5 = ((f32[32,1,256]{2,1,0:T(1,128)}), f32[32,1,256]{2,1,0:T(1,128)S(1)}, u32[]{:S(2)}, u32[]{:S(2)}) async-start(f32[32,1,256]{2,1,0:T(1,128)} %broadcast_in_dim.13), calls=%async_computation.8 | async-start | bytes 65536 | tf_op jit(solution)/shard_map/all_to_all | solution.py:18
  267.5 90.4 %all-gather.7.cloned.1.call-start = ((), (), s32[]{:S(2)}) async-start(), calls=%async_computation.17 | async-start | bytes 1892352 | tf_op jit(solution)/shard_map/all_gather | solution.py:143
  291.2 68.8 %copy-start.4 = (bf16[3584,224]{0,1:T(8,128)(2,1)S(1)}, bf16[3584,224]{0,1:T(8,128)(2,1)}, u32[]{:S(2)}) copy-start(bf16[3584,224]{0,1:T(8,128)(2,1)} %param.19) | copy-start | bytes 4816900
  291.2 68.8 %copy-start.8 = (f32[256,224]{0,1:T(8,128)S(1)}, f32[256,224]{0,1:T(8,128)}, u32[]{:S(2)}) copy-start(f32[256,224]{0,1:T(8,128)} %copy-done.7) | copy-start | bytes 688132
  357.9 2.2 copy-start.13
  360.1 1.4 copy-start.6
  360.1 1.4 copy-start.9
  364.5 26.8 %all-to-all-start.7 = ((bf16[32,256,112]{1,2,0:T(8,128)(2,1)}), bf16[32,256,112]{1,2,0:T(8,128)(2,1)S(1)}, u32[]{:S(2)}, u32[]{:S(2)}) async-start(bf16[32,256,112]{1,2,0:T(8,128)(2,1)} %bitcast.16), calls=%async_computation.10 | async-start | bytes 3670016 | tf_op jit(solution)/shard_map/all_to_all | solution.py:42
  368.6 40.3 %copy-start.16 = (bf16[1,256,112]{1,2,0:T(8,128)(2,1)S(1)}, bf16[1,256,112]{1,2,0:T(8,128)(2,1)}, u32[]{:S(2)}) copy-start(bf16[1,256,112]{1,2,0:T(8,128)(2,1)} %reduce-scatter.8.cloned.1.call-done) | copy-start | bytes 172036
  368.6 108.5 %copy-start.15 = (f32[256,1024]{1,0:T(8,128)S(1)}, f32[256,1024]{1,0:T(8,128)}, u32[]{:S(2)}) copy-start(f32[256,1024]{1,0:T(8,128)} %get-tuple-element.5) | copy-start | bytes 3145732
  368.6 108.5 %all-gather.9.cloned.1.call-start = ((), (), s32[]{:S(2)}) async-start(), calls=%async_computation.18 | async-start | bytes 1892352 | tf_op jit(solution)/shard_map/all_gather | solution.py:160
  410.6 157.7 %all-gather.11.cloned.1.call-start = ((), (), s32[]{:S(2)}) async-start(), calls=%async_computation.19 | async-start | bytes 5242880 | tf_op jit(solution)/shard_map/all_gather | solution.py:81
  477.1 5.8 copy-start.11
  482.9 1.9 copy-start.3
  528.8 37.1 %all-to-all-start.9 = ((bf16[256,4,896]{0,2,1:T(8,128)(2,1)}), bf16[256,4,896]{0,2,1:T(8,128)(2,1)S(1)}, u32[]{:S(2)}, u32[]{:S(2)}) async-start(bf16[256,4,896]{0,2,1:T(8,128)(2,1)} %bitcast.60), calls=%async_computation.12 | async-start | bytes 3670016 | tf_op jit(solution)/shard_map/all_to_all | solution.py:167
  568.3 5.9 %copy-start.14 = (bf16[4,256,896]{2,1,0:T(8,128)(2,1)S(1)}, bf16[4,256,896]{2,1,0:T(8,128)(2,1)}, u32[]{:S(2)}) copy-start(bf16[4,256,896]{2,1,0:T(8,128)(2,1)} %copy.48) | copy-start | bytes 5505028
  568.3 5.9 %copy-start.20 = (bf16[1024,2048]{1,0:T(8,128)(2,1)S(1)}, bf16[1024,2048]{1,0:T(8,128)(2,1)}, u32[]{:S(2)}) copy-start(bf16[1024,2048]{1,0:T(8,128)(2,1)} %all-gather.11.cloned.1.call-done) | copy-start | bytes 12582916
  574.2 3.4 copy-start.1
Sparse Core Ops, SparseCore 0:
  11.7 71.2 all-gather.4
  190.2 29.3 reduce-scatter.3
  222.0 19.4 reduce-scatter.5
  243.7 15.2 reduce-scatter.7
  291.3 66.5 all-gather.6
  410.7 66.3 all-gather.8
  484.2 72.1 all-gather.10
where the time goes:
time: 586 us; the launch traced here: 584 us
  waiting for transfers between devices  351 us (60%)
  blocking collectives  119 us (20%)
  matrix products  36.9 us (6%)
  local copies, waits for them, and re-layouts  23.7 us (4%)
  starting transfers between devices  20.1 us (3%)
  other arithmetic  19.1 us (3%)
  between operations  14.5 us (2%)
    all_gather x1, waiting for transfers between devices, per_device(): centered = lax.all_gather(centered_share, TENSOR_LATENT, axis=1, tiled=True)  72.6 us
    reduce_scatter x3, waiting for transfers between devices, sum_in_order(): pieces = lax.psum_scatter(pieces, axes[k], scatter_dimension=0, tiled=True)  68.8 us
    all_gather x1, waiting for transfers between devices, per_device(): grad_output = lax.all_gather(grad_share, TENSOR_LATENT, axis=1, tiled=True)  66.7 us
    all_gather x1, waiting for transfers between devices, per_device(): grad_recon = lax.all_gather(recon_share, TENSOR_LATENT, axis=1, tiled=True)  66.5 us
    all_to_all x1, blocking collectives, per_device(): lax.all_to_all(centered, 'batch', split_axis=1, concat_axis=0, tiled=True)  44 us
    all_to_all x3, blocking collectives, copy_for_each(): return lax.all_to_all(copies, axis, split_axis=0, concat_axis=0, tiled=True)  39.4 us
    all_to_all x1, waiting for transfers between devices, per_device(): lax.all_to_all(grad_recon, 'batch', split_axis=1, concat_axis=0, tiled=True)  28.5 us
    all_to_all x2, waiting for transfers between devices, copy_for_each(): return lax.all_to_all(copies, axis, split_axis=0, concat_axis=0, tiled=True)  25.4 us
  transfers between devices with their start and end apart: 11, of which 10 were waited for; matrix products, arithmetic and copies ran while one was open for 1% of the time, Pallas kernels for 0%

commit v1 on v0

--- a/solution.py
+++ b/solution.py
@@ -1,3 +1,4 @@
+import functools
 import jax
 import jax.numpy as jnp
 from jax import lax
@@ -6,6 +7,22 @@
 
 TENSOR_LATENT = ("tensor_0", "tensor_1", "latent")
 epsilon = 1e-06
+
+
+def run_the_zones(local_x, dimension_no):
+    lower = jnp.concatenate(
+        lax.all_to_all(
+            jnp.stack(lax.psum(1, axis_name=TENSOR_LATENT) * [local_x]),
+            axis_name=TENSOR_LATENT,
+            split_axis=0,
+            concat_axis=0,
+        ),
+        axis=dimension_no,
+    )
+    return lower
+
+
+_replace_ports = functools.partial(run_the_zones, dimension_no=1)
 
 
 def rows_for(lines, count):
@@ -140,7 +157,7 @@
     grad_normed = grad_result * second_share
     inner_out = over_copies(jnp.sum(grad_normed * normed_out, axis=1), TENSOR_LATENT) / model_width
     grad_share = (scale_out * (grad_normed - normed_out * inner_out[:, None])).astype(bf16)
-    grad_output = lax.all_gather(grad_share, TENSOR_LATENT, axis=1, tiled=True)
+    grad_output = _replace_ports(grad_share)
     grad_hidden = lax.dot_general(
         grad_output, down_weight, contract_last, preferred_element_type=f32
     )

time: 586 us -> 547 us (0.933)
  waiting for transfers between devices: 351 us -> 285 us
  blocking collectives: 119 us -> 145 us
    all_gather x1 -> x0, waiting for transfers between devices: 66.7 us -> none  [per_device(): grad_output = lax.all_gather(grad_share, TENSOR_LATENT, axis=1, tiled=True)]
    all_to_all x0 -> x1, blocking collectives: none -> 26.4 us  [run_the_zones(): lax.all_to_all(jnp.stack(lax.psum(1, axis_name=TENSOR_LATENT) * [local_x]...]
  transfers between devices with their start and end apart: 11 -> 10, of which waited for: 10 -> 9; matrix products, arithmetic and copies ran while one was open for 1% -> 1% of each run, Pallas kernels for 0% -> 0%
where the time goes in v1:
time: 547 us; the launch traced here: 546 us
  waiting for transfers between devices  285 us (52%)
  blocking collectives  145 us (27%)
  matrix products  35.3 us (6%)
  local copies, waits for them, and re-layouts  24.7 us (5%)
  starting transfers between devices  23.3 us (4%)
  other arithmetic  18.5 us (3%)
  between operations  14.4 us (3%)
    all_gather x1, waiting for transfers between devices, per_device(): centered = lax.all_gather(centered_share, TENSOR_LATENT, axis=1, tiled=True)  72.6 us
    reduce_scatter x3, waiting for transfers between devices, sum_in_order(): pieces = lax.psum_scatter(pieces, axes[k], scatter_dimension=0, tiled=True)  68.8 us
    all_gather x1, waiting for transfers between devices, per_device(): grad_recon = lax.all_gather(recon_share, TENSOR_LATENT, axis=1, tiled=True)  65.9 us
    all_to_all x1, blocking collectives, per_device(): lax.all_to_all(centered, 'batch', split_axis=1, concat_axis=0, tiled=True)  44 us
    all_to_all x3, blocking collectives, copy_for_each(): return lax.all_to_all(copies, axis, split_axis=0, concat_axis=0, tiled=True)  38.8 us
    all_to_all x1, waiting for transfers between devices, per_device(): lax.all_to_all(grad_recon, 'batch', split_axis=1, concat_axis=0, tiled=True)  28.5 us
    all_to_all x1, blocking collectives, run_the_zones(): lax.all_to_all(jnp.stack(lax.psum(1, axis_name=TENSOR_LATENT) * [local_x]...  26.4 us
    all_to_all x2, waiting for transfers between devices, copy_for_each(): return lax.all_to_all(copies, axis, split_axis=0, concat_axis=0, tiled=True)  25.5 us
  transfers between devices with their start and end apart: 10, of which 9 were waited for; matrix products, arithmetic and copies ran while one was open for 1% of the time, Pallas kernels for 0%

profile of v1, /device:TPU:1, one launch (start us, length us, event | category | flops | bytes accessed | tf_op | source)
XLA Modules:
  0.0 545.7 jit_solution(12142428231570238576)
XLA Ops:
  7.2 0.9 dynamic_slice.12
  8.1 1.5 subtract_convert_fusion
  9.7 0.7 convert_element_type.91
  10.3 72.6 %all-gather.4.cloned.1.call-done = bf16[256,3584]{0,1:T(8,128)(2,1)} async-done(((bf16[256,112]{0,1:T(8,128)(2,1)}), bf16[256,3584]{0,1:T(8,128)(2,1)}) %all-gather.4.cloned.1.call-update) | async-done | bytes 1835024 | tf_op jit(solution)/shard_map/all_gather | solution.py:130
  82.9 6.7 %maximum_convert_fusion = (bf16[256,1024]{1,0:T(8,128)(2,1)S(1)}, f32[256,1024]{1,0:T(8,128)}) fusion(f32[1024]{0:T(1024)S(1)} %convert_element_type.91, bf16[256,3584]{0,1:T(8,128)(2,1)} %all-gather.4.cloned.1.call-done, bf16[3584,1024]{1,0:T(8,128)(2,1)} %param.13), kind=kOutput, calls=%fused_computation.20 | convolution fusion | flops 1879834624 | bytes 10752000 | tf_op jit(solution)/shard_map/dot_general | solution.py:131
  89.7 5.3 convolution_convert_fusion
  95.0 0.1 copy.69
  95.2 23.6 %all_to_all.86 = bf16[4,8,8,3584]{3,2,1,0:T(8,128)(2,1)S(1)} all-to-all(bf16[4,8,8,3584]{3,2,1,0:T(8,128)(2,1)S(1)} %bitcast.61), channel_id=1, replica_groups=mesh['batch'=4,'tensor_0'=4,'tensor_1'=2,'latent'=4] {'latent'}, dimensions={0} | all-to-all | bytes 3670016 | tf_op jit(solution)/shard_map/all_to_all | solution.py:59
  118.8 1.1 reduce_sum.98
  119.9 11.9 %all_to_all.87 = bf16[8,8,3584]{2,1,0:T(8,128)(2,1)S(1)} all-to-all(bf16[8,8,3584]{2,1,0:T(8,128)(2,1)} %reduce_sum.98), channel_id=1, replica_groups=mesh['batch'=4,'tensor_0'=4,'tensor_1'=2,'latent'=4] {'tensor_0','tensor..., dimensions={0} | all-to-all | bytes 917504 | tf_op jit(solution)/shard_map/all_to_all | solution.py:67
  131.9 11.1 %all_to_all.88 = bf16[8,8,3584]{2,1,0:T(8,128)(2,1)S(1)} all-to-all(bf16[8,8,3584]{2,1,0:T(8,128)(2,1)S(1)} %broadcast_in_dim.11), channel_id=1, replica_groups=mesh['batch'=4,'tensor_0'=4,'tensor_1'=2,'latent'=4] {'tensor_0','tensor..., dimensions={0} | all-to-all | bytes 917504 | tf_op jit(solution)/shard_map/all_to_all | solution.py:35
  143.1 1.4 broadcast_in_dim.12
  144.4 3.7 all-to-all-start.4
  148.2 17.5 %all-to-all-done.4 = bf16[4,8,8,3584]{3,2,1,0:T(8,128)(2,1)S(1)} async-done(((bf16[4,8,8,3584]{3,2,1,0:T(8,128)(2,1)}), bf16[4,8,8,3584]{3,2,1,0:T(8,128)(2,1)S(1)}, u32[]{:S(2)}, u32[]{:S(2)}) %all-to-all-start.4) | async-done | bytes 1835040 | tf_op jit(solution)/shard_map/all_to_all | solution.py:35
  165.8 2.2 copy_convert_fusion
  168.0 5.1 copy.54
  173.1 4.4 broadcast_add_fusion
  177.5 0.6 multiply_reduce_fusion
  178.1 0.1 rsqrt.20
  178.2 3.5 fusion.51
  181.7 0.1 copy-done.2
  181.8 0.5 copy-done.5
  182.3 0.8 fusion.52
  183.1 0.7 copy-done.11
  183.8 1.9 convolution_convert_fusion.1
  185.7 2.9 copy.55
  188.6 1.4 copy.56
  190.1 29.4 %reduce-scatter.4.cloned.1.call-done = bf16[8,256,112]{1,2,0:T(8,128)(2,1)} async-done(((bf16[32,256,112]{1,2,0:T(8,128)(2,1)}), bf16[8,256,112]{1,2,0:T(8,128)(2,1)}) %reduce-scatter.4.cloned.1.call-update) | async-done | bytes 458768 | tf_op jit(solution)/shard_map/reduce_scatter | solution.py:83
  219.6 21.8 %reduce-scatter.6.cloned.1.call-done = bf16[2,256,112]{1,2,0:T(8,128)(2,1)} async-done(((bf16[8,256,112]{1,2,0:T(8,128)(2,1)}), bf16[2,256,112]{1,2,0:T(8,128)(2,1)}) %reduce-scatter.6.cloned.1.call-update) | async-done | bytes 114704 | tf_op jit(solution)/shard_map/reduce_scatter | solution.py:83
  241.4 17.6 %reduce-scatter.8.cloned.1.call-done = bf16[1,256,112]{1,2,0:T(8,128)(2,1)} async-done(((bf16[2,256,112]{1,2,0:T(8,128)(2,1)}), bf16[1,256,112]{1,2,0:T(8,128)(2,1)}) %reduce-scatter.8.cloned.1.call-update) | async-done | bytes 57360 | tf_op jit(solution)/shard_map/reduce_scatter | solution.py:83
  259.0 0.8 fusion.28
  259.9 0.6 broadcast_in_dim.13
  260.5 7.0 %all-to-all-start.5 = ((f32[32,1,256]{2,1,0:T(1,128)}), f32[32,1,256]{2,1,0:T(1,128)S(1)}, u32[]{:S(2)}, u32[]{:S(2)}) async-start(f32[32,1,256]{2,1,0:T(1,128)} %broadcast_in_dim.13), calls=%async_computation.8 | async-start | bytes 65536 | tf_op jit(solution)/shard_map/all_to_all | solution.py:35
  267.5 0.8 broadcast_multiply_fusion.2
  268.3 8.0 %all-to-all-done.5 = f32[32,1,256]{2,1,0:T(1,128)S(1)} async-done(((f32[32,1,256]{2,1,0:T(1,128)}), f32[32,1,256]{2,1,0:T(1,128)S(1)}, u32[]{:S(2)}, u32[]{:S(2)}) %all-to-all-start.5) | async-done | bytes 32800 | tf_op jit(solution)/shard_map/all_to_all | solution.py:35
  276.3 1.1 fusion.24
  277.4 12.1 %all_to_all.89 = f32[32,1,256]{2,1,0:T(1,128)S(1)} all-to-all(f32[32,1,256]{2,1,0:T(1,128)S(1)} %broadcast_in_dim.14), channel_id=1, replica_groups=mesh['batch'=4,'tensor_0'=4,'tensor_1'=2,'latent'=4] {'tensor_0','tensor..., dimensions={0} | all-to-all | bytes 65536 | tf_op jit(solution)/shard_map/all_to_all | solution.py:35
  289.5 1.0 fusion.27
  290.6 0.1 stack.2
  290.7 26.4 %all_to_all.90 = bf16[32,256,112]{1,2,0:T(8,128)(2,1)S(1)} all-to-all(bf16[32,256,112]{1,2,0:T(8,128)(2,1)S(1)} %stack.2), channel_id=1, replica_groups=mesh['batch'=4,'tensor_0'=4,'tensor_1'=2,'latent'=4] {'tensor_0','tensor..., dimensions={0} | all-to-all | bytes 3670016 | tf_op jit(solution)/shard_map/all_to_all | solution.py:14
  317.1 0.6 fusion.53
  317.6 0.8 copy-done.4
  318.5 0.8 fusion.29
  319.4 0.6 copy-done.6
  320.0 0.7 fusion
  320.7 2.3 copy.59
  322.9 7.4 %all-to-all-start.8 = ((bf16[32,256,112]{1,2,0:T(8,128)(2,1)}), bf16[32,256,112]{1,2,0:T(8,128)(2,1)S(1)}, u32[]{:S(2)}, u32[]{:S(2)}) async-start(bf16[32,256,112]{1,2,0:T(8,128)(2,1)} %bitcast.18), calls=%async_computation.11 | async-start | bytes 3670016 | tf_op jit(solution)/shard_map/all_to_all | solution.py:59
  330.4 0.1 dynamic_slice.15
  330.5 23.4 %all-to-all-done.8 = bf16[32,256,112]{1,2,0:T(8,128)(2,1)S(1)} async-done(((bf16[32,256,112]{1,2,0:T(8,128)(2,1)}), bf16[32,256,112]{1,2,0:T(8,128)(2,1)S(1)}, u32[]{:S(2)}, u32[]{:S(2)}) %all-to-all-start.8) | async-done | bytes 1835040 | tf_op jit(solution)/shard_map/all_to_all | solution.py:59
  353.9 0.3 convert_reduce_fusion
  354.1 1.0 multiply_reduce_fusion.1
  355.2 15.6 %all_to_all.91 = f32[32,1,256]{2,1,0:T(1,128)S(1)} all-to-all(f32[32,1,256]{2,1,0:T(1,128)S(1)} %broadcast_in_dim.15), channel_id=1, replica_groups=mesh['batch'=4,'tensor_0'=4,'tensor_1'=2,'latent'=4] {'tensor_0','tensor..., dimensions={0} | all-to-all | bytes 65536 | tf_op jit(solution)/shard_map/all_to_all | solution.py:35
  370.8 1.6 add_convert_fusion
  372.5 65.9 %all-gather.6.cloned.1.call-done = bf16[256,3584]{0,1:T(8,128)(2,1)} async-done(((bf16[256,112]{0,1:T(8,128)(2,1)}), bf16[256,3584]{0,1:T(8,128)(2,1)}) %all-gather.6.cloned.1.call-update) | async-done | bytes 1835024 | tf_op jit(solution)/shard_map/all_gather | solution.py:177
  438.4 5.8 %fusion.11 = bf16[256,1024]{1,0:T(8,128)(2,1)S(1)} fusion(bf16[256,3584]{0,1:T(8,128)(2,1)} %all-gather.6.cloned.1.call-done, bf16[1024,3584]{1,0:T(8,128)(2,1)} %param.15, f32[256,1024]{1,0:T(8,128)S(1)} %copy-done.14), kind=kOutput, calls=%fused_computation.18 | convolution fusion | flops 1879834624 | bytes 10747904 | tf_op jit(solution)/shard_map/dot_general | solution.py:178
  444.2 1.1 pad_maximum_fusion
  445.3 0.8 copy-done.3
  446.1 44.0 %all_to_all.92 = bf16[256,4,896]{0,2,1:T(8,128)(2,1)} all-to-all(bf16[256,4,896]{0,2,1:T(8,128)(2,1)S(1)} %bitcast.57), channel_id=1, replica_groups=mesh['batch'=4,'tensor_0'=4,'tensor_1'=2,'latent'=4] {'batch'}, dimensions={1} | all-to-all | bytes 3670016 | tf_op jit(solution)/shard_map/all_to_all | solution.py:183
  490.1 5.0 all-to-all-start.10
  495.1 3.5 copy.51
  498.7 28.5 %all-to-all-done.10 = bf16[256,4,896]{0,2,1:T(8,128)(2,1)S(1)} async-done(((bf16[256,4,896]{0,2,1:T(8,128)(2,1)}), bf16[256,4,896]{0,2,1:T(8,128)(2,1)S(1)}, u32[]{:S(2)}, u32[]{:S(2)}) %all-to-all-start.10) | async-done | bytes 1835040 | tf_op jit(solution)/shard_map/all_to_all | solution.py:184
  527.2 2.4 copy.61
  529.6 5.9 %fusion.8 = bf16[1024,896]{1,0:T(8,128)(2,1)} fusion(bf16[1024,896]{1,0:T(8,128)(2,1)} %bitcast.66, bf16[1024,2048]{1,0:T(8,128)(2,1)} %all-gather.8.cloned.1.call-done), kind=kOutput, calls=%fused_computation.15 | convolution fusion | flops 1879965696 | bytes 5767168 | tf_op jit(solution)/shard_map/dot_general | solution.py:190
  535.5 3.4 fusion.5
  (60 shorter events, 0.8 us)
Async XLA Ops:
  7.2 176.6 %copy-start = (bf16[224,3584]{1,0:T(8,128)(2,1)S(1)}, bf16[224,3584]{1,0:T(8,128)(2,1)}, u32[]{:S(2)}) copy-start(bf16[224,3584]{1,0:T(8,128)(2,1)} %param.21) | copy-start | bytes 4816900
  7.2 75.8 %all-gather.4.cloned.1.call-start = ((), (), s32[]{:S(2)}) async-start(), calls=%async_computation.14 | async-start | bytes 1892352 | tf_op jit(solution)/shard_map/all_gather | solution.py:130
  89.7 5.4 copy-start.9
  144.4 3.8 copy-start.17
  144.4 3.8 copy-start.18
  144.4 21.3 %all-to-all-start.4 = ((bf16[4,8,8,3584]{3,2,1,0:T(8,128)(2,1)}), bf16[4,8,8,3584]{3,2,1,0:T(8,128)(2,1)S(1)}, u32[]{:S(2)}, u32[]{:S(2)}) async-start(bf16[4,8,8,3584]{3,2,1,0:T(8,128)(2,1)} %broadcast_in_dim.12), calls=%async_computation.4 | async-start | bytes 3670016 | tf_op jit(solution)/shard_map/all_to_all | solution.py:35
  148.2 71.4 %reduce-scatter.4.cloned.1.call-start = ((), (), s32[]{:S(2)}) async-start(), calls=%async_computation.15 | async-start | bytes 2293760 | tf_op jit(solution)/shard_map/reduce_scatter | solution.py:83
  178.2 3.6 copy-start.2
  178.2 4.1 copy-start.5
  182.3 0.8 copy-start.7
  183.1 0.7 copy-start.11
  190.0 86.3 %copy-start.16 = (bf16[256,112]{0,1:T(8,128)(2,1)S(1)}, bf16[256,112]{0,1:T(8,128)(2,1)}, u32[]{:S(2)}) copy-start(bf16[256,112]{0,1:T(8,128)(2,1)} %param.12) | copy-start | bytes 172036
  190.1 51.3 %reduce-scatter.6.cloned.1.call-start = ((), (), s32[]{:S(2)}) async-start(), calls=%async_computation.16 | async-start | bytes 573440 | tf_op jit(solution)/shard_map/reduce_scatter | solution.py:83
  219.6 39.5 %reduce-scatter.8.cloned.1.call-start = ((), (), s32[]{:S(2)}) async-start(), calls=%async_computation.17 | async-start | bytes 172032 | tf_op jit(solution)/shard_map/reduce_scatter | solution.py:83
  260.5 15.7 %all-to-all-start.5 = ((f32[32,1,256]{2,1,0:T(1,128)}), f32[32,1,256]{2,1,0:T(1,128)S(1)}, u32[]{:S(2)}, u32[]{:S(2)}) async-start(f32[32,1,256]{2,1,0:T(1,128)} %broadcast_in_dim.13), calls=%async_computation.8 | async-start | bytes 65536 | tf_op jit(solution)/shard_map/all_to_all | solution.py:35
  317.0 1.4 copy-start.4
  317.1 1.4 copy-start.8
  317.1 1.5 copy-start.12
  318.5 1.4 copy-start.6
  322.9 31.0 %all-to-all-start.8 = ((bf16[32,256,112]{1,2,0:T(8,128)(2,1)}), bf16[32,256,112]{1,2,0:T(8,128)(2,1)S(1)}, u32[]{:S(2)}, u32[]{:S(2)}) async-start(bf16[32,256,112]{1,2,0:T(8,128)(2,1)} %bitcast.18), calls=%async_computation.11 | async-start | bytes 3670016 | tf_op jit(solution)/shard_map/all_to_all | solution.py:59
  330.3 40.5 %copy-start.15 = (bf16[1,256,112]{1,2,0:T(8,128)(2,1)S(1)}, bf16[1,256,112]{1,2,0:T(8,128)(2,1)}, u32[]{:S(2)}) copy-start(bf16[1,256,112]{1,2,0:T(8,128)(2,1)} %reduce-scatter.8.cloned.1.call-done) | copy-start | bytes 172036
  330.3 108.1 %copy-start.14 = (f32[256,1024]{1,0:T(8,128)S(1)}, f32[256,1024]{1,0:T(8,128)}, u32[]{:S(2)}) copy-start(f32[256,1024]{1,0:T(8,128)} %get-tuple-element.5) | copy-start | bytes 3145732
  330.4 108.1 %all-gather.6.cloned.1.call-start = ((), (), s32[]{:S(2)}) async-start(), calls=%async_computation.18 | async-start | bytes 1892352 | tf_op jit(solution)/shard_map/all_gather | solution.py:177
  372.5 157.1 %all-gather.8.cloned.1.call-start = ((), (), s32[]{:S(2)}) async-start(), calls=%async_computation.19 | async-start | bytes 5242880 | tf_op jit(solution)/shard_map/all_gather | solution.py:98
  438.4 5.8 %copy-start.10 = (bf16[256,1024]{1,0:T(8,128)(2,1)S(1)}, bf16[256,1024]{1,0:T(8,128)(2,1)}, u32[]{:S(2)}) copy-start(bf16[256,1024]{1,0:T(8,128)(2,1)} %copy-done.9) | copy-start | bytes 1572868
  444.2 1.9 copy-start.3
  490.1 37.1 %all-to-all-start.10 = ((bf16[256,4,896]{0,2,1:T(8,128)(2,1)}), bf16[256,4,896]{0,2,1:T(8,128)(2,1)S(1)}, u32[]{:S(2)}, u32[]{:S(2)}) async-start(bf16[256,4,896]{0,2,1:T(8,128)(2,1)} %bitcast.64), calls=%async_computation.13 | async-start | bytes 3670016 | tf_op jit(solution)/shard_map/all_to_all | solution.py:184
  529.6 5.9 %copy-start.13 = (bf16[4,256,896]{2,1,0:T(8,128)(2,1)S(1)}, bf16[4,256,896]{2,1,0:T(8,128)(2,1)}, u32[]{:S(2)}) copy-start(bf16[4,256,896]{2,1,0:T(8,128)(2,1)} %copy.51) | copy-start | bytes 5505028
  529.6 5.9 %copy-start.19 = (bf16[1024,2048]{1,0:T(8,128)(2,1)S(1)}, bf16[1024,2048]{1,0:T(8,128)(2,1)}, u32[]{:S(2)}) copy-start(bf16[1024,2048]{1,0:T(8,128)(2,1)} %all-gather.8.cloned.1.call-done) | copy-start | bytes 12582916
  535.5 3.4 copy-start.1
Sparse Core Ops, SparseCore 0:
  11.7 71.2 all-gather.3
  190.2 29.3 reduce-scatter.3
  222.0 19.3 reduce-scatter.5
  243.7 15.3 reduce-scatter.7
  372.6 65.7 all-gather.5
  445.5 72.1 all-gather.7
